TPU v7x, 128 devices: a whole 4x4x4 slice. The times are simulated.
128 devices in a mesh: row: 16 (over y_lo, x, core), col: 8 (over y_hi, z).
Axes of the slice: x: 4, y: 4 (y_hi: 2, y_lo: 2; y = y_hi * 2 + y_lo), z: 4, core: 2. Of those that a mesh axis runs over, the one named last changes fastest.
Arguments:
- embeddings: float32 [49152, 64], P(('row', 'col')), may hold values from -6 to 6
- inv_length: float32 [64], replicated, may hold values from 0.1 to 0.4
- noise: float32 [49152], P(('row', 'col')), may hold values from 0.1 to 1
- probes: bfloat16 [49152, 256], P(('row', 'col')), may hold values from -1.5 to 1.5
Outputs:
- applied: float32 [49152, 256], P(('row', 'col'))
All inputs are finite; a program needn't handle non-finite values.
Results may differ from a plain program's by a relative error of at most 0.0029.
Values may be sent and summed in bfloat16 or wider, within the bound.
No kernel may reach another device: no remote copies, remote signals or barrier semaphores. Data moves between devices by JAX's collectives and lax.ppermute only.
A program may use at most 192 MiB of HBM per device.

v0:
```python
import jax
import jax.numpy as jnp
from jax import lax
from jax.sharding import PartitionSpec as P


def kernel_tile(rows, row_sq, cols, col_sq, col_probes):
    gram = jnp.dot(
        rows, cols.T, precision=lax.Precision.HIGHEST, preferred_element_type=jnp.float32
    )
    dist = row_sq[:, None] + col_sq[None, :] - 2.0 * gram
    kernel = jnp.exp(-0.5 * dist).astype(jnp.bfloat16)
    return jnp.dot(kernel, col_probes, preferred_element_type=jnp.float32)


def on_device(embeddings, inv_length, noise, probes):
    scaled = embeddings * inv_length[None, :]
    own_sq = jnp.sum(scaled * scaled, axis=1)
    diag_term = noise[:, None] * probes.astype(jnp.float32)
    every = lax.all_gather(scaled, ("row", "col"), axis=0, tiled=True)
    every_sq = jnp.sum(every * every, axis=1)
    product = kernel_tile(
        scaled, own_sq, every, every_sq, lax.all_gather(probes, ("row", "col"), axis=0, tiled=True)
    )
    return product + diag_term


def solution(mesh):
    return jax.shard_map(
        on_device,
        mesh=mesh,
        in_specs=(P(("row", "col"), None), P(), P(("row", "col")), P(("row", "col"), None)),
        out_specs=P(("row", "col"), None),
        check_vma=False,
    )
```

profile of v0, /device:TPU:1, one launch (start us, length us, event | category | flops | bytes accessed | tf_op | source)
XLA Modules:
  0.0 696.6 jit_solution(2096074242026698704)
XLA Ops:
  6.5 0.0 all-gather.3.cloned.1.call-start
  6.5 1.6 multiply_reduce_fusion.1
  8.2 0.0 all-gather.3.cloned.1.call-update
  8.2 0.0 all-gather.5.cloned.1.call-start
  8.2 0.7 all-gather.5.cloned.1.call-update
  8.9 321.8 %all-gather.3.cloned.1.call-done = f32[49152,64]{0,1:T(8,128)} async-done(((f32[384,64]{0,1:T(8,128)}), f32[49152,64]{0,1:T(8,128)}) %all-gather.3.cloned.1.call-update) | async-done | bytes 12582928 | tf_op jit(solution)/shard_map/all_gather | solution.py:20
  330.7 5.8 multiply_reduce_fusion
  336.5 0.0 copy-start
  336.5 0.0 copy-start.1
  336.5 77.5 %exponential_convert_fusion = bf16[384,49152]{1,0:T(8,128)(2,1)} fusion(f32[384,64]{0,1:T(8,128)} %get-tuple-element.6, f32[49152,64]{0,1:T(8,128)} %all-gather.3.cloned.1.call-done, f32[49152]{0:T(1024)S(1)} %multiply_reduce_fusion, f32[384]{0:T(512)S(1)} %get-tuple-element.5), kind=kOutput, calls=%fused_computation | convolution fusion | flops 14589886464 | bytes 50628096 | tf_op jit(solution)/shard_map/dot_general | solution.py:8
  414.1 251.7 %all-gather.5.cloned.1.call-done = bf16[49152,256]{1,0:T(8,128)(2,1)} async-done(((bf16[384,256]{1,0:T(8,128)(2,1)}), bf16[49152,256]{1,0:T(8,128)(2,1)}) %all-gather.5.cloned.1.call-update) | async-done | bytes 25165840 | tf_op jit(solution)/shard_map/all_gather | solution.py:23
  665.8 0.0 copy-done
  665.8 0.0 copy-done.1
  665.8 24.0 %convolution_add_fusion = f32[384,256]{1,0:T(8,128)} fusion(bf16[384,49152]{1,0:T(8,128)(2,1)} %exponential_convert_fusion, bf16[49152,256]{1,0:T(8,128)(2,1)} %all-gather.5.cloned.1.call-done, bf16[384,256]{1,0:T(8,128)(2,1)S(1)} %copy-done, f32[384]{0:T(512)S(1)} %copy-done.1), kind=kOutput, calls=%fused_computation.2 | convolution fusion | flops 9663971328 | bytes 63505920 | tf_op jit(solution)/shard_map/dot_general | solution.py:13
Async XLA Ops:
  6.5 324.2 %all-gather.3.cloned.1.call-start = ((), (), s32[]{:S(2)}) async-start(), calls=%async_computation | async-start | bytes 12681216 | tf_op jit(solution)/shard_map/all_gather | solution.py:20
  8.2 657.6 %all-gather.5.cloned.1.call-start = ((), (), s32[]{:S(2)}) async-start(), calls=%async_computation.1 | async-start | bytes 25362432 | tf_op jit(solution)/shard_map/all_gather | solution.py:23
  336.5 329.3 %copy-start = (bf16[384,256]{1,0:T(8,128)(2,1)S(1)}, bf16[384,256]{1,0:T(8,128)(2,1)}, u32[]{:S(2)}) copy-start(bf16[384,256]{1,0:T(8,128)(2,1)} %param.7) | copy-start | bytes 589828
  336.5 329.2 %copy-start.1 = (f32[384]{0:T(512)S(1)}, f32[384]{0:T(512)}, u32[]{:S(2)}) copy-start(f32[384]{0:T(512)} %param.6) | copy-start | bytes 4612
Sparse Core Ops, SparseCore 0:
  9.0 321.6 all-gather.2
  332.4 333.2 all-gather.4
where the time goes:
time: 697 us
  waiting for transfers between devices  574 us (82%)
  matrix products  102 us (15%)
  between operations  13.4 us (2%)
  other arithmetic  7.37 us (1%)
    all_gather x1, waiting for transfers between devices, on_device(): every = lax.all_gather(scaled, ('row', 'col'), axis=0, tiled=True)  322 us
    all_gather x1, waiting for transfers between devices, on_device(): lax.all_gather(probes, ('row', 'col'), axis=0, tiled=True)  252 us
    dot_general x1, matrix products, kernel_tile(): jnp.dot(rows, cols.T, precision=lax.Precision.HIGHEST, preferred_element_...  77.5 us
    dot_general x1, matrix products, kernel_tile(): return jnp.dot(kernel, col_probes, preferred_element_type=jnp.float32)  24 us
  transfers between devices with their start and end apart: 2, of which 2 were waited for; matrix products, arithmetic and copies ran while one was open for 12% of the time, Pallas kernels for 0%

commit v1 on v0

--- a/solution.py
+++ b/solution.py
@@ -2,6 +2,11 @@
 import jax.numpy as jnp
 from jax import lax
 from jax.sharding import PartitionSpec as P
+
+
+def gather_over(block, axis, dim):
+    stack = jnp.stack([block] * lax.axis_size(axis))
+    return jnp.concatenate(lax.all_to_all(stack, axis, 0, 0), axis=dim)
 
 
 def kernel_tile(rows, row_sq, cols, col_sq, col_probes):
@@ -17,7 +22,7 @@
     scaled = embeddings * inv_length[None, :]
     own_sq = jnp.sum(scaled * scaled, axis=1)
     diag_term = noise[:, None] * probes.astype(jnp.float32)
-    every = lax.all_gather(scaled, ("row", "col"), axis=0, tiled=True)
+    every = gather_over(scaled, ("row", "col"), 0)
     every_sq = jnp.sum(every * every, axis=1)
     product = kernel_tile(
         scaled, own_sq, every, every_sq, lax.all_gather(probes, ("row", "col"), axis=0, tiled=True)

time: 697 us -> 506 us (0.73)
  waiting for transfers between devices: 574 us -> 202 us
  blocking collectives: 0 us -> 167 us
  local copies, waits for them, and re-layouts: 0.01 us -> 11.5 us
    all_gather x1 -> x0, waiting for transfers between devices: 322 us -> none  [on_device(): every = lax.all_gather(scaled, ('row', 'col'), axis=0, tiled=True)]
    all_to_all x0 -> x1, blocking collectives: none -> 167 us  [gather_over(): return jnp.concatenate(lax.all_to_all(stack, axis, 0, 0), axis=dim)]
    all_gather x1, waiting for transfers between devices: 252 us -> 202 us  [on_device(): lax.all_gather(probes, ('row', 'col'), axis=0, tiled=True)]
    reshape x0 -> x1, local copies, waits for them, and re-layouts: none -> 9.89 us  [gather_over(): return jnp.concatenate(lax.all_to_all(stack, axis, 0, 0), axis=dim)]
  transfers between devices with their start and end apart: 2 -> 1, of which waited for: 2 -> 1; matrix products, arithmetic and copies ran while one was open for 12% -> 19% of each run, Pallas kernels for 0% -> 0%
where the time goes in v1:
time: 506 us; the launch traced here: 504 us
  waiting for transfers between devices  202 us (40%)
  blocking collectives  167 us (33%)
  matrix products  102 us (20%)
  between operations  13.4 us (3%)
  local copies, waits for them, and re-layouts  11.5 us (2%)
  other arithmetic  7.86 us (2%)
    all_gather x1, waiting for transfers between devices, on_device(): lax.all_gather(probes, ('row', 'col'), axis=0, tiled=True)  202 us
    all_to_all x1, blocking collectives, gather_over(): return jnp.concatenate(lax.all_to_all(stack, axis, 0, 0), axis=dim)  167 us
    dot_general x1, matrix products, kernel_tile(): jnp.dot(rows, cols.T, precision=lax.Precision.HIGHEST, preferred_element_...  77.7 us
    dot_general x1, matrix products, kernel_tile(): return jnp.dot(kernel, col_probes, preferred_element_type=jnp.float32)  24 us
  transfers between devices with their start and end apart: 1, of which 1 were waited for; matrix products, arithmetic and copies ran while one was open for 19% of the time, Pallas kernels for 0%

profile of v1, /device:TPU:1, one launch (start us, length us, event | category | flops | bytes accessed | tf_op | source)
XLA Modules:
  0.0 504.0 jit_solution(4785490584450723699)
XLA Ops:
  6.5 0.0 all-gather.2.cloned.1.call-start
  6.5 0.7 all-gather.2.cloned.1.call-update
  7.3 1.0 multiply_reduce_fusion.1
  8.2 1.6 stack.2
  9.8 167.0 %all_to_all.5 = f32[128,384,64]{1,2,0:T(8,128)} all-to-all(f32[128,384,64]{1,2,0:T(8,128)S(1)} %stack.2), channel_id=1, replica_groups=mesh['row'=16,'col'=8] {'row','col'}, dimensions={0} | all-to-all | bytes 25165824 | tf_op jit(solution)/shard_map/all_to_all | solution.py:9
  176.9 9.9 %copy.7 = f32[128,8,8,384]{3,2,0,1:T(8,128)} copy(f32[128,8,8,384]{3,2,1,0:T(8,128)} %bitcast.6) | data formatting | bytes 25165824 | tf_op jit(solution)/shard_map/reshape | solution.py:9
  186.7 6.9 %multiply_reduce_fusion = f32[128,384]{1,0:T(8,128)S(1)} fusion(f32[128,384,64]{1,2,0:T(8,128)} %all_to_all.5), kind=kLoop, calls=%fused_computation.1 | loop fusion | flops 6242304 | bytes 12779520 | tf_op jit(solution)/shard_map/reduce_sum | solution.py:26
  193.6 0.0 copy-start
  193.7 0.0 copy-start.1
  193.7 77.7 %exponential_convert_fusion = bf16[384,49152]{1,0:T(8,128)(2,1)} fusion(f32[384,64]{0,1:T(8,128)S(1)} %get-tuple-element.6, f32[49152,64]{0,1:T(8,128)} %bitcast.7, f32[49152]{0:T(1024)S(1)} %add.19, f32[384]{0:T(512)S(1)} %get-tuple-element.5), kind=kOutput, calls=%fused_computation | convolution fusion | flops 14589886464 | bytes 50628096 | tf_op jit(solution)/shard_map/dot_general | solution.py:13
  271.4 201.7 %all-gather.2.cloned.1.call-done = bf16[49152,256]{1,0:T(8,128)(2,1)} async-done(((bf16[384,256]{1,0:T(8,128)(2,1)}), bf16[49152,256]{1,0:T(8,128)(2,1)}) %all-gather.2.cloned.1.call-update) | async-done | bytes 25165840 | tf_op jit(solution)/shard_map/all_gather | solution.py:28
  473.1 0.0 copy-done
  473.1 0.0 copy-done.1
  473.1 24.0 %convolution_add_fusion = f32[384,256]{1,0:T(8,128)} fusion(bf16[384,49152]{1,0:T(8,128)(2,1)} %exponential_convert_fusion, bf16[49152,256]{1,0:T(8,128)(2,1)} %all-gather.2.cloned.1.call-done, bf16[384,256]{1,0:T(8,128)(2,1)S(1)} %copy-done, f32[384]{0:T(512)S(1)} %copy-done.1), kind=kOutput, calls=%fused_computation.2 | convolution fusion | flops 9663971328 | bytes 63505920 | tf_op jit(solution)/shard_map/dot_general | solution.py:18
  (1 shorter events, 0.0 us)
Async XLA Ops:
  6.5 466.5 %all-gather.2.cloned.1.call-start = ((), (), s32[]{:S(2)}) async-start(), calls=%async_computation.1 | async-start | bytes 25362432 | tf_op jit(solution)/shard_map/all_gather | solution.py:28
  193.6 279.4 %copy-start = (bf16[384,256]{1,0:T(8,128)(2,1)S(1)}, bf16[384,256]{1,0:T(8,128)(2,1)}, u32[]{:S(2)}) copy-start(bf16[384,256]{1,0:T(8,128)(2,1)} %param.7) | copy-start | bytes 589828
  193.7 279.4 %copy-start.1 = (f32[384]{0:T(512)S(1)}, f32[384]{0:T(512)}, u32[]{:S(2)}) copy-start(f32[384]{0:T(512)} %param.6) | copy-start | bytes 4612
Sparse Core Ops, SparseCore 0:
  9.0 464.0 all-gather.1
